TPU v7x, 256 devices: a whole 4x4x8 slice. The times are simulated.
256 devices in a mesh: rows: 8 (over x, core), protos: 32 (over y, z).
Axes of the slice: x: 4, y: 4, z: 8, core: 2. Of those that a mesh axis runs over, the one named last changes fastest.
Arguments:
- teacher_features: bfloat16 [4096, 384], P(('rows', 'protos')), may hold values from -80 to 80, as said below
- student_features: bfloat16 [4096, 384], P(('rows', 'protos')), may hold values from -80 to 80, as said below
- prototypes: bfloat16 [131072, 384], P('protos'), may hold values from -80 to 80, as said below
Outputs:
- feature_grad: float32 [4096, 384], P(('rows', 'protos'))
- proto_grad: float32 [8, 16384, 384], P('rows', 'protos')
Inputs may be any that keep to these rules, and one draw needn't show every extreme that they name: `teacher_features`: every row has nonzero entries. `student_features`: every row has nonzero entries. `prototypes`: every row has nonzero entries.
All inputs are finite; a program needn't handle non-finite values.
Results may differ from a plain program's by a relative error of at most 0.012.
The roundings to bfloat16 on the way count: a program that leaves them out, or rounds other values in their place, can miss the bound.
Values may be sent and summed in bfloat16 or wider, within the bound.
A program may use at most 64 MiB of HBM per device.

v0:
```python
import math
import jax
import jax.numpy as jnp
from jax import lax
from jax.sharding import PartitionSpec as P

D = 384
K = 131072
PASSES = 3
eps = 1e-06


def unitize(values):
    values = values.astype(jnp.float32)
    return (values * lax.rsqrt(jnp.sum(values * values, axis=1, keepdims=True) + eps)).astype(
        jnp.bfloat16
    )


def against(left, right):
    return lax.dot_general(
        left, right, (((1,), (1,)), ((), ())), preferred_element_type=jnp.float32
    )


def on_device(teacher_features, student_features, prototypes):
    scale = 1.5 * math.sqrt(D)
    unit_w = unitize(prototypes)
    local_t = unitize(teacher_features)
    local_s = unitize(student_features)
    unit_t, unit_s = (
        lax.all_gather(local_t, "protos", axis=0, tiled=True),
        lax.all_gather(local_s, "protos", axis=0, tiled=True),
    )
    kernel = jnp.exp(scale * against(unit_t, unit_w))
    powers = jnp.exp(scale * against(unit_s, unit_w))
    student_part = jnp.sum(powers, axis=1)
    student_whole = lax.psum(student_part, "protos")
    row_scale = jnp.ones((kernel.shape[0],), jnp.float32)
    col_scale = jnp.ones((kernel.shape[1],), jnp.float32)
    for step in range(PASSES):
        col_part = jnp.dot(row_scale, kernel, precision=lax.Precision.HIGHEST)
        col_scale = 1.0 / lax.psum(col_part, "rows")
        row_part = jnp.dot(kernel, col_scale, precision=lax.Precision.HIGHEST)
        if step == 0:
            row_whole = lax.psum(row_part, "protos")
        else:
            row_whole = lax.psum(row_part, "protos")
        row_scale = 1.0 / row_whole
    target = kernel * row_scale[:, None] * col_scale[None, :]
    probs = powers / student_whole[:, None]
    delta = (probs - target).astype(jnp.bfloat16)
    feature_term = scale * jnp.dot(delta, unit_w, preferred_element_type=jnp.float32)
    feature_grad = lax.psum_scatter(feature_term, "protos", scatter_dimension=0, tiled=True)
    row_groups = lax.axis_size("rows")
    total_rows = delta.shape[0] * row_groups
    factor = scale * K / total_rows
    block = delta.shape[1] // row_groups
    term = factor * lax.dot_general(
        delta, unit_s, (((0,), (0,)), ((), ())), preferred_element_type=jnp.float32
    )
    proto_grad = lax.psum_scatter(
        term.reshape(row_groups, block, term.shape[1]), "rows", scatter_dimension=0, tiled=True
    )
    return (feature_grad, proto_grad)


def solution(mesh):
    return jax.shard_map(
        on_device,
        mesh=mesh,
        in_specs=(P(("rows", "protos"), None), P(("rows", "protos"), None), P("protos", None)),
        out_specs=(P(("rows", "protos"), None), P("rows", "protos", None)),
        check_vma=False,
    )
```

profile of v0, /device:TPU:1, one launch (start us, length us, event | category | flops | bytes accessed | tf_op | source)
XLA Modules:
  0.0 735.6 jit_solution(5828482277272511359)
XLA Ops:
  7.2 0.0 reduce-scatter.3.cloned.1.call-start
  7.2 0.8 fusion.5
  8.0 0.8 fusion.3
  8.9 0.8 fusion.4
  9.7 0.8 fusion.6
  10.4 2.6 fusion.1
  13.0 0.0 copy-start.3
  13.1 41.6 %all_gather.6 = bf16[512,384]{1,0:T(8,128)(2,1)S(1)} all-gather(bf16[16,384]{1,0:T(8,128)(2,1)S(1)} %fusion.4), channel_id=1, replica_groups=mesh['rows'=8,'protos'=32] {'protos'}, dimensions={0}, use_global_device_ids=true | all-gather | bytes 405504 | tf_op jit(solution)/shard_map/all_gather | solution.py:33
  54.6 36.7 %all_gather.7 = bf16[512,384]{1,0:T(8,128)(2,1)S(1)} all-gather(bf16[16,384]{1,0:T(8,128)(2,1)S(1)} %fusion.6), channel_id=1, replica_groups=mesh['rows'=8,'protos'=32] {'protos'}, dimensions={0}, use_global_device_ids=true | all-gather | bytes 405504 | tf_op jit(solution)/shard_map/all_gather | solution.py:32
  91.3 4.3 multiply_exponential_fusion
  95.7 0.0 copy-start
  95.7 3.2 copy-done
  98.9 4.0 fusion.7
  102.9 0.0 copy-done.3
  102.9 44.7 %psum.50 = f32[4096]{0:T(1024)S(1)} all-reduce(f32[4096]{0:T(1024)S(1)} %bitcast.34), channel_id=1, replica_groups=mesh['rows'=8,'protos'=32] {'rows'}, use_global_device_ids=true, to_apply=%region_5.0 | all-reduce | flops 4096 | bytes 32768 | tf_op jit(solution)/shard_map/psum | solution.py:43
  147.7 9.4 %fusion.14 = f32[1,512]{1,0:T(1,128)S(1)} fusion(f32[512,4096]{1,0:T(8,128)} %copy-done, f32[4096,1]{0,1:T(1,128)S(1)} %bitcast.30), kind=kOutput, calls=%fused_computation.31 | convolution fusion | flops 25165824 | bytes 8407040 | tf_op jit(solution)/shard_map/dot_general | solution.py:44
  157.1 58.6 %psum.51 = f32[512]{0:T(512)S(1)} all-reduce(f32[512]{0:T(512)S(1)} %bitcast.36), channel_id=1, replica_groups=mesh['rows'=8,'protos'=32] {'protos'}, use_global_device_ids=true, to_apply=%region_6.0 | all-reduce | flops 512 | bytes 4096 | tf_op jit(solution)/shard_map/psum | solution.py:46
  215.7 6.3 fusion.15
  222.1 37.4 %psum.52 = f32[4096]{0:T(1024)S(1)} all-reduce(f32[4096]{0:T(1024)S(1)} %bitcast.31), channel_id=1, replica_groups=mesh['rows'=8,'protos'=32] {'rows'}, use_global_device_ids=true, to_apply=%region_7.0 | all-reduce | flops 4096 | bytes 32768 | tf_op jit(solution)/shard_map/psum | solution.py:43
  259.5 9.4 %fusion.16 = f32[1,512]{1,0:T(1,128)S(1)} fusion(f32[512,4096]{1,0:T(8,128)} %copy-done, f32[4096,1]{0,1:T(1,128)S(1)} %bitcast.32), kind=kOutput, calls=%fused_computation.33 | convolution fusion | flops 25165824 | bytes 8407040 | tf_op jit(solution)/shard_map/dot_general | solution.py:44
  268.9 55.8 %psum.53 = f32[512]{0:T(512)S(1)} all-reduce(f32[512]{0:T(512)S(1)} %bitcast.38), channel_id=1, replica_groups=mesh['rows'=8,'protos'=32] {'protos'}, use_global_device_ids=true, to_apply=%region_8.0 | all-reduce | flops 512 | bytes 4096 | tf_op jit(solution)/shard_map/psum | solution.py:48
  324.7 0.0 copy-start.1
  324.7 6.5 fusion.17
  331.2 37.6 %psum.54 = f32[4096]{0:T(1024)} all-reduce(f32[4096]{0:T(1024)S(1)} %bitcast.33), channel_id=1, replica_groups=mesh['rows'=8,'protos'=32] {'rows'}, use_global_device_ids=true, to_apply=%region_9.0 | all-reduce | flops 4096 | bytes 32768 | tf_op jit(solution)/shard_map/psum | solution.py:43
  368.8 0.7 broadcast_divide_fusion
  369.6 10.0 %fusion.18 = f32[1,512]{1,0:T(1,128)} fusion(f32[512,4096]{1,0:T(8,128)} %copy-done, f32[4096,1]{0,1:T(1,128)S(1)} %bitcast.29), kind=kOutput, calls=%fused_computation.35 | convolution fusion | flops 25165824 | bytes 8407040 | tf_op jit(solution)/shard_map/dot_general | solution.py:44
  379.6 0.0 copy-done.1
  379.6 6.2 fusion
  385.8 58.2 %all-reduce = (f32[512]{0:T(512)}, f32[512]{0:T(512)}) all-reduce(f32[512]{0:T(512)} %bitcast.35, f32[512]{0:T(512)} %get-tuple-element.4), channel_id=1, replica_groups=mesh['rows'=8,'protos'=32] {'protos'}, use_global_device_ids=true, to_apply=%region_10.0 | all-reduce | flops 1024 | bytes 8192 | tf_op jit(solution)/shard_map/psum | solution.py:48
  444.0 0.7 broadcast_divide_fusion.5
  444.6 0.0 copy-start.4
  444.6 7.3 subtract_convert_fusion
  452.0 0.0 copy-start.2
  452.0 2.0 copy-done.2
  454.0 0.0 copy-done.4
  454.0 3.3 convolution_multiply_fusion.1
  457.4 0.0 reduce-scatter.3.cloned.1.call-update
  457.4 0.0 reduce-scatter.5.cloned.1.call-start
  457.4 7.2 convolution_multiply_fusion
  464.7 0.0 reduce-scatter.5.cloned.1.call-update
  464.7 212.9 %reduce-scatter.3.cloned.1.call-done = f32[16,384]{1,0:T(8,128)} async-done(((f32[512,384]{1,0:T(8,128)}), f32[16,384]{1,0:T(8,128)}) %reduce-scatter.3.cloned.1.call-update) | async-done | bytes 24592 | tf_op jit(solution)/shard_map/reduce_scatter | solution.py:54
  677.6 51.2 %reduce-scatter.5.cloned.1.call-done = f32[1,512,384]{2,1,0:T(8,128)} async-done(((f32[8,512,384]{2,1,0:T(8,128)}), f32[1,512,384]{2,1,0:T(8,128)}) %reduce-scatter.5.cloned.1.call-update) | async-done | bytes 786448 | tf_op jit(solution)/shard_map/reduce_scatter | solution.py:62
  (7 shorter events, 0.0 us)
Async XLA Ops:
  7.2 670.4 %reduce-scatter.3.cloned.1.call-start = ((), (), s32[]{:S(2)}) async-start(), calls=%async_computation.2 | async-start | bytes 811008 | tf_op jit(solution)/shard_map/reduce_scatter | solution.py:54
  13.0 89.9 %copy-start.3 = (f32[4096]{0:T(1024)}, f32[4096]{0:T(1024)S(1)}, u32[]{:S(2)}) copy-start(f32[4096]{0:T(1024)S(1)} %add_rsqrt_fusion) | copy-start | bytes 49156
  95.7 3.2 copy-start
  324.7 54.9 %copy-start.1 = (bf16[4096,384]{1,0:T(8,128)(2,1)S(1)}, bf16[4096,384]{1,0:T(8,128)(2,1)}, u32[]{:S(2)}) copy-start(bf16[4096,384]{1,0:T(8,128)(2,1)} %param.5) | copy-start | bytes 9437188
  444.6 9.4 %copy-start.4 = (f32[4096]{0:T(1024)S(1)}, f32[4096]{0:T(1024)}, u32[]{:S(2)}) copy-start(f32[4096]{0:T(1024)} %copy-done.3) | copy-start | bytes 49156
  452.0 2.0 copy-start.2
  457.4 271.4 %reduce-scatter.5.cloned.1.call-start = ((), (), s32[]{:S(2)}) async-start(), calls=%async_computation.3 | async-start | bytes 7077888 | tf_op jit(solution)/shard_map/reduce_scatter | solution.py:62
Sparse Core Ops, SparseCore 0:
  457.5 220.0 reduce-scatter.2
  680.7 48.0 reduce-scatter.4
where the time goes:
time: 736 us
  blocking collectives  371 us (50%)
  waiting for transfers between devices  264 us (36%)
  matrix products  66.9 us (9%)
  other arithmetic  14.6 us (2%)
  between operations  14.1 us (2%)
    reduce_scatter x1, waiting for transfers between devices, on_device(): lax.psum_scatter(feature_term, 'protos', scatter_dimension=0, tiled=True)  213 us
    psum x3, blocking collectives, on_device(): row_whole = lax.psum(row_part, 'protos')  173 us
    psum x3, blocking collectives, on_device(): col_scale = 1.0 / lax.psum(col_part, 'rows')  120 us
    reduce_scatter x1, waiting for transfers between devices, on_device(): lax.psum_scatter(term.reshape(row_groups, block, term.shape[1]), 'rows',...  51.2 us
    all_gather x1, blocking collectives, on_device(): lax.all_gather(local_s, 'protos', axis=0, tiled=True)  41.6 us
    all_gather x1, blocking collectives, on_device(): lax.all_gather(local_t, 'protos', axis=0, tiled=True)  36.7 us
    dot_general x3, matrix products, on_device(): row_part = jnp.dot(kernel, col_scale, precision=lax.Precision.HIGHEST)  28.9 us
    dot_general x3, matrix products, on_device(): col_part = jnp.dot(row_scale, kernel, precision=lax.Precision.HIGHEST)  16.9 us
  transfers between devices with their start and end apart: 2, of which 2 were waited for; matrix products, arithmetic and copies ran while one was open for 1% of the time, Pallas kernels for 0%

commit v1 on v0

--- a/solution.py
+++ b/solution.py
@@ -45,7 +45,7 @@
         if step == 0:
             row_whole = lax.psum(row_part, "protos")
         else:
-            row_whole = lax.psum(row_part, "protos")
+            row_whole = jnp.sum(lax.all_gather(row_part, "protos"), axis=0)
         row_scale = 1.0 / row_whole
     target = kernel * row_scale[:, None] * col_scale[None, :]
     probs = powers / student_whole[:, None]

time: 736 us -> 705 us (0.958)
  blocking collectives: 371 us -> 335 us
    psum x3 -> x1, blocking collectives: 173 us -> 58.8 us  [on_device(): row_whole = lax.psum(row_part, 'protos')]
    all_gather x0 -> x2, blocking collectives: none -> 77.2 us  [on_device(): row_whole = jnp.sum(lax.all_gather(row_part, 'protos'), axis=0)]
where the time goes in v1:
time: 705 us; the launch traced here: 704 us
  blocking collectives  335 us (48%)
  waiting for transfers between devices  265 us (38%)
  matrix products  66.6 us (9%)
  other arithmetic  18.4 us (3%)
  between operations  14.1 us (2%)
    reduce_scatter x1, waiting for transfers between devices, on_device(): lax.psum_scatter(feature_term, 'protos', scatter_dimension=0, tiled=True)  214 us
    psum x3, blocking collectives, on_device(): col_scale = 1.0 / lax.psum(col_part, 'rows')  120 us
    all_gather x2, blocking collectives, on_device(): row_whole = jnp.sum(lax.all_gather(row_part, 'protos'), axis=0)  77.2 us
    psum x1, blocking collectives, on_device(): row_whole = lax.psum(row_part, 'protos')  58.8 us
    reduce_scatter x1, waiting for transfers between devices, on_device(): lax.psum_scatter(term.reshape(row_groups, block, term.shape[1]), 'rows',...  51.2 us
    all_gather x1, blocking collectives, on_device(): lax.all_gather(local_s, 'protos', axis=0, tiled=True)  41.6 us
    all_gather x1, blocking collectives, on_device(): lax.all_gather(local_t, 'protos', axis=0, tiled=True)  36.7 us
    dot_general x3, matrix products, on_device(): row_part = jnp.dot(kernel, col_scale, precision=lax.Precision.HIGHEST)  28.9 us
  transfers between devices with their start and end apart: 2, of which 2 were waited for; matrix products, arithmetic and copies ran while one was open for 1% of the time, Pallas kernels for 0%

profile of v1, /device:TPU:1, one launch (start us, length us, event | category | flops | bytes accessed | tf_op | source)
XLA Modules:
  0.0 704.2 jit_solution(11898373398884908829)
XLA Ops:
  7.2 0.0 reduce-scatter.3.cloned.1.call-start
  7.2 0.8 fusion.5
  8.0 0.8 fusion.3
  8.9 0.8 fusion.4
  9.7 0.8 fusion.6
  10.4 2.6 fusion.1
  13.0 0.0 copy-start.3
  13.1 41.6 %all_gather.18 = bf16[512,384]{1,0:T(8,128)(2,1)S(1)} all-gather(bf16[16,384]{1,0:T(8,128)(2,1)S(1)} %fusion.4), channel_id=1, replica_groups=mesh['rows'=8,'protos'=32] {'protos'}, dimensions={0}, use_global_device_ids=true | all-gather | bytes 405504 | tf_op jit(solution)/shard_map/all_gather | solution.py:33
  54.6 36.7 %all_gather.19 = bf16[512,384]{1,0:T(8,128)(2,1)S(1)} all-gather(bf16[16,384]{1,0:T(8,128)(2,1)S(1)} %fusion.6), channel_id=1, replica_groups=mesh['rows'=8,'protos'=32] {'protos'}, dimensions={0}, use_global_device_ids=true | all-gather | bytes 405504 | tf_op jit(solution)/shard_map/all_gather | solution.py:32
  91.3 4.3 multiply_exponential_fusion
  95.7 0.0 copy-start
  95.7 3.2 copy-done
  98.9 0.0 copy-start.1
  98.9 4.6 fusion.7
  103.5 45.3 %psum.36 = f32[4096]{0:T(1024)} all-reduce(f32[4096]{0:T(1024)} %bitcast.40), channel_id=1, replica_groups=mesh['rows'=8,'protos'=32] {'rows'}, use_global_device_ids=true, to_apply=%region_5.0 | all-reduce | flops 4096 | bytes 32768 | tf_op jit(solution)/shard_map/psum | solution.py:43
  148.9 0.7 broadcast_divide_fusion.2
  149.6 10.0 %fusion.14 = f32[1,512]{1,0:T(1,128)} fusion(f32[512,4096]{1,0:T(8,128)} %copy-done, f32[4096,1]{0,1:T(1,128)S(1)} %bitcast.36), kind=kOutput, calls=%fused_computation.33 | convolution fusion | flops 25165824 | bytes 8407040 | tf_op jit(solution)/shard_map/dot_general | solution.py:44
  159.6 0.0 copy-done.3
  159.6 0.0 copy-done.1
  159.6 5.5 fusion
  165.1 58.8 %all-reduce = (f32[512]{0:T(512)S(1)}, f32[512]{0:T(512)}) all-reduce(f32[512]{0:T(512)} %bitcast.41, f32[512]{0:T(512)} %get-tuple-element.4), channel_id=1, replica_groups=mesh['rows'=8,'protos'=32] {'protos'}, use_global_device_ids=true, to_apply=%region_6.0 | all-reduce | flops 1024 | bytes 8192 | tf_op jit(solution)/shard_map/psum | solution.py:46
  223.9 6.3 fusion.15
  230.3 38.3 %psum.38 = f32[4096]{0:T(1024)} all-reduce(f32[4096]{0:T(1024)S(1)} %bitcast.37), channel_id=1, replica_groups=mesh['rows'=8,'protos'=32] {'rows'}, use_global_device_ids=true, to_apply=%region_7.0 | all-reduce | flops 4096 | bytes 32768 | tf_op jit(solution)/shard_map/psum | solution.py:43
  268.6 0.7 broadcast_divide_fusion.1
  269.3 9.4 %convolution_bitcast_fusion.1 = f32[1,1,512]{2,1,0:T(1,128)S(1)} fusion(f32[512,4096]{1,0:T(8,128)} %copy-done, f32[4096,1]{0,1:T(1,128)S(1)} %bitcast.38), kind=kOutput, calls=%fused_computation.11 | convolution fusion | flops 25165824 | bytes 8407040 | tf_op jit(solution)/shard_map/dot_general | solution.py:44
  278.7 37.8 %all-gather.2 = f32[32,1,512]{2,1,0:T(1,128)} all-gather(f32[1,1,512]{2,1,0:T(1,128)S(1)} %convolution_bitcast_fusion.1), channel_id=2, replica_groups=mesh['rows'=8,'protos'=32] {'protos'}, dimensions={0}, use_global_device_ids=true | all-gather | bytes 67584 | tf_op jit(solution)/shard_map/all_gather | solution.py:48
  316.6 0.9 reduce_sum.58
  317.5 6.3 fusion.16
  323.8 36.6 %psum.39 = f32[4096]{0:T(1024)} all-reduce(f32[4096]{0:T(1024)S(1)} %bitcast.39), channel_id=1, replica_groups=mesh['rows'=8,'protos'=32] {'rows'}, use_global_device_ids=true, to_apply=%region_9.0 | all-reduce | flops 4096 | bytes 32768 | tf_op jit(solution)/shard_map/psum | solution.py:43
  360.4 0.7 broadcast_divide_fusion
  361.2 9.4 %convolution_bitcast_fusion = f32[1,1,512]{2,1,0:T(1,128)S(1)} fusion(f32[512,4096]{1,0:T(8,128)} %copy-done, f32[4096,1]{0,1:T(1,128)S(1)} %bitcast.35), kind=kOutput, calls=%fused_computation.10 | convolution fusion | flops 25165824 | bytes 8407040 | tf_op jit(solution)/shard_map/dot_general | solution.py:44
  370.6 39.4 %all-gather.3 = f32[32,1,512]{2,1,0:T(1,128)} all-gather(f32[1,1,512]{2,1,0:T(1,128)S(1)} %convolution_bitcast_fusion), channel_id=3, replica_groups=mesh['rows'=8,'protos'=32] {'protos'}, dimensions={0}, use_global_device_ids=true | all-gather | bytes 67584 | tf_op jit(solution)/shard_map/all_gather | solution.py:48
  410.0 1.5 reduce_sum.59
  411.5 0.7 broadcast_divide_fusion.5
  412.1 0.0 copy-start.4
  412.1 7.3 %subtract_convert_fusion = bf16[512,4096]{1,0:T(8,128)(2,1)S(1)} fusion(f32[512,4096]{1,0:T(8,128)} %copy-done, f32[512,4096]{1,0:T(8,128)} %get-tuple-element.5, f32[4096]{0:T(1024)S(1)} %broadcast_divide_fusion, f32[512]{0:T(512)S(1)} %broadcast_divide_fusion.5, f32[512]{0:T(512)} %get-tuple-element.3), kind=kLoop, calls=%fused_computation | loop fusion | flops 12582912 | bytes 20992000 | tf_op jit(solution)/shard_map/convert_element_type | solution.py:52
  419.5 0.0 copy-start.2
  419.5 2.0 copy-done.2
  421.5 0.0 copy-done.4
  421.5 3.3 convolution_multiply_fusion.1
  424.8 0.0 reduce-scatter.3.cloned.1.call-update
  424.9 0.0 reduce-scatter.5.cloned.1.call-start
  424.9 7.2 %convolution_multiply_fusion = f32[4096,384]{1,0:T(8,128)} fusion(bf16[512,4096]{1,0:T(8,128)(2,1)} %copy-done.2, bf16[512,384]{1,0:T(8,128)(2,1)S(1)} %all_gather.18), kind=kOutput, calls=%fused_computation.8 | convolution fusion | flops 1612185600 | bytes 10878976 | tf_op jit(solution)/shard_map/dot_general | solution.py:59
  432.1 0.0 reduce-scatter.5.cloned.1.call-update
  432.2 214.1 %reduce-scatter.3.cloned.1.call-done = f32[16,384]{1,0:T(8,128)} async-done(((f32[512,384]{1,0:T(8,128)}), f32[16,384]{1,0:T(8,128)}) %reduce-scatter.3.cloned.1.call-update) | async-done | bytes 24592 | tf_op jit(solution)/shard_map/reduce_scatter | solution.py:54
  646.2 51.2 %reduce-scatter.5.cloned.1.call-done = f32[1,512,384]{2,1,0:T(8,128)} async-done(((f32[8,512,384]{2,1,0:T(8,128)}), f32[1,512,384]{2,1,0:T(8,128)}) %reduce-scatter.5.cloned.1.call-update) | async-done | bytes 786448 | tf_op jit(solution)/shard_map/reduce_scatter | solution.py:62
  (5 shorter events, 0.0 us)
Async XLA Ops:
  7.2 639.0 %reduce-scatter.3.cloned.1.call-start = ((), (), s32[]{:S(2)}) async-start(), calls=%async_computation.2 | async-start | bytes 811008 | tf_op jit(solution)/shard_map/reduce_scatter | solution.py:54
  13.0 146.6 %copy-start.3 = (f32[4096]{0:T(1024)}, f32[4096]{0:T(1024)S(1)}, u32[]{:S(2)}) copy-start(f32[4096]{0:T(1024)S(1)} %add_rsqrt_fusion) | copy-start | bytes 49156
  95.7 3.2 copy-start
  98.9 60.7 %copy-start.1 = (bf16[4096,384]{1,0:T(8,128)(2,1)S(1)}, bf16[4096,384]{1,0:T(8,128)(2,1)}, u32[]{:S(2)}) copy-start(bf16[4096,384]{1,0:T(8,128)(2,1)} %param.5) | copy-start | bytes 9437188
  412.1 9.4 %copy-start.4 = (f32[4096]{0:T(1024)S(1)}, f32[4096]{0:T(1024)}, u32[]{:S(2)}) copy-start(f32[4096]{0:T(1024)} %copy-done.3) | copy-start | bytes 49156
  419.5 2.0 copy-start.2
  424.9 272.5 %reduce-scatter.5.cloned.1.call-start = ((), (), s32[]{:S(2)}) async-start(), calls=%async_computation.3 | async-start | bytes 7077888 | tf_op jit(solution)/shard_map/reduce_scatter | solution.py:62
Sparse Core Ops, SparseCore 0:
  425.0 221.1 reduce-scatter.2
  649.3 48.0 reduce-scatter.4
